TPU v7x, 128 devices: a whole 4x4x4 slice. The times are simulated.
128 devices in a mesh: row: 16 (over x, y), col: 8 (over z, core).
Axes of the slice: x: 4, y: 4, z: 4, core: 2. Of those that a mesh axis runs over, the one named last changes fastest.
Arguments:
- orbitals: bfloat16 [131072, 512], P(('row', 'col')), may hold values from -6 to 6
- coulomb: bfloat16 [32768, 32768], P('row', 'col'), may hold values from -0.0014648438 to 0.0014648438
- interp: bfloat16 [131072, 1024], P(('row', 'col')), may hold values from -0.1875 to 0.1875
- box_counts: int32 [128], replicated, may hold values from 1 to 768, 32768 in all
- owner_map: int32 [32768], replicated, may hold values from 0 to 32767, as said below
- grid_rows: int32 [128, 1024], P(('row', 'col')), may hold values from 0 to 1023, each once within a row
- listed: int32 [128, 1024], P(('row', 'col')), may hold values from 0 to 255
Outputs:
- exchange_action: float32 [131072, 512], P(('row', 'col'))
Inputs may be any that keep to these rules, and one draw needn't show every extreme that they name: `box_counts`: the counts sum to 32768; the largest is exactly 768. `owner_map`: A permutation of the 32768 positions; a point's owner is position // 256. No box holds more than 6 points of one owner, and the box with 768 points holds exactly 6 of some owner. `grid_rows`: each row is a permutation.
All inputs are finite; a program needn't handle non-finite values.
Results may differ from a plain program's by a relative error of at most 0.012.
Values may be sent and summed in bfloat16 or wider, within the bound.
A program may use at most 128 MiB of HBM per device.

v0:
```python
import jax
import jax.numpy as jnp
from jax import lax
from jax.sharding import PartitionSpec as P

NORB = 512
LIST = 1024
OWN = 256
SLOTS = 768


def copy_for_each(x, axis):
    copies = jnp.broadcast_to(x, (lax.axis_size(axis), *x.shape))
    return lax.all_to_all(copies, axis, split_axis=0, concat_axis=0, tiled=True)


def in_order(parts, dim):
    parts = jnp.moveaxis(parts, 0, dim)
    dims = parts.shape
    return parts.reshape(*dims[:dim], dims[dim] * dims[dim + 1], *dims[dim + 2 :])


def gather_directly(x, axis, dim):
    parts = copy_for_each(x, axis)
    return in_order(parts, dim)


def add_block(shard_rows, left_rows, kernel_tile):
    pair_tile = jnp.einsum(
        "ak,bk->ab", left_rows, shard_rows, preferred_element_type=jnp.float32
    ).astype(jnp.bfloat16)
    weighted = (pair_tile.astype(jnp.float32) * kernel_tile.astype(jnp.float32)).astype(
        jnp.bfloat16
    )
    return jnp.dot(weighted, shard_rows, preferred_element_type=jnp.float32)


def shards(orbitals, coulomb, interp, box_counts, owner_map, grid_rows, listed):
    row_count = lax.axis_size("row")
    col_count = lax.axis_size("col")
    box_total = row_count * col_count
    point_total = OWN * box_total
    capacity = (SLOTS + box_total - 1) // box_total
    per_owner = LIST // box_total
    my_box = lax.axis_index("row") * col_count + lax.axis_index("col")
    box_ids = jnp.arange(box_total, dtype=jnp.int32)
    first_point = jnp.sum(jnp.where(box_ids < my_box, box_counts, 0))
    my_count = jnp.sum(jnp.where(box_ids == my_box, box_counts, 0))
    slot_ids = jnp.arange(SLOTS, dtype=jnp.int32)
    is_live = slot_ids < my_count
    listing = jnp.minimum(first_point + slot_ids, point_total - 1)
    owner_ids = owner_map[listing] // OWN
    matches = (
        (owner_ids[:, None] == owner_ids[None, :])
        & is_live[None, :]
        & (slot_ids[None, :] < slot_ids[:, None])
    )
    pair_rank = jnp.sum(matches.astype(jnp.int32), axis=1)
    target = jnp.where(is_live, owner_ids * capacity + pair_rank, box_total * capacity)
    dest_slots = jnp.arange(box_total * capacity, dtype=jnp.int32)
    hits = target[None, :] == dest_slots[:, None]
    source_slot = jnp.sum(jnp.where(hits, slot_ids[None, :], 0), axis=1)
    filled = jnp.any(hits, axis=1)
    picked = orbitals[grid_rows[0, source_slot]]
    outgoing = jnp.where(filled[:, None], picked, jnp.zeros_like(picked))
    received = lax.all_to_all(
        outgoing.reshape(box_total, capacity, NORB),
        ("row", "col"),
        split_axis=0,
        concat_axis=0,
        tiled=True,
    )
    received = received.reshape(box_total * capacity, NORB)
    wanted_pos = my_box * OWN + jnp.arange(OWN, dtype=jnp.int32)
    all_listing = jnp.arange(point_total, dtype=jnp.int32)
    my_points = jnp.sum(
        jnp.where(owner_map[None, :] == wanted_pos[:, None], all_listing[None, :], 0), axis=1
    )
    box_ends = jnp.cumsum(box_counts)
    source = jnp.sum((my_points[:, None] >= box_ends[None, :]).astype(jnp.int32), axis=1)
    earlier = (source[:, None] == source[None, :]) & (my_points[None, :] < my_points[:, None])
    source_rank = jnp.sum(earlier.astype(jnp.int32), axis=1)
    owned_rows = received[source * capacity + source_rank]
    left_rows = gather_directly(owned_rows, "col", 0)
    partial_sums = add_block(
        lax.all_gather(owned_rows, "row", axis=0, tiled=True), left_rows, coulomb
    )
    owned_result = lax.psum_scatter(partial_sums, "col", scatter_dimension=0, tiled=True).astype(
        jnp.bfloat16
    )
    wanted = listed[0].reshape(box_total, per_owner)
    fetched = lax.all_to_all(
        owned_result[
            lax.all_to_all(wanted, ("row", "col"), split_axis=0, concat_axis=0, tiled=True)
        ],
        ("row", "col"),
        split_axis=0,
        concat_axis=0,
        tiled=True,
    )
    chosen_rows = fetched.reshape(LIST, NORB)
    return -jnp.dot(interp, chosen_rows, preferred_element_type=jnp.float32)


def solution(mesh):
    return jax.shard_map(
        shards,
        mesh=mesh,
        in_specs=(
            P(("row", "col"), None),
            P("row", "col"),
            P(("row", "col"), None),
            P(),
            P(),
            P(("row", "col"), None),
            P(("row", "col"), None),
        ),
        out_specs=P(("row", "col"), None),
        check_vma=False,
    )
```

profile of v0, /device:TPU:1, one launch (start us, length us, event | category | flops | bytes accessed | tf_op | source)
XLA Modules:
  0.0 216.9 jit_solution(2038270782259860773)
XLA Ops:
  6.5 1.5 fusion.12
  8.1 0.7 fusion.7
  8.8 4.7 %gather_fusion = s32[768]{0:T(1024)S(1)} fusion(s32[32768]{0:T(1024)} %param.11, s32[1024]{0:T(1024)S(1)} %pad_clamp_fusion.2), kind=kCustom, calls=%fused_computation | custom fusion | bytes 9216 | tf_op jit(solution)/shard_map/gather | solution.py:52
  13.5 0.7 iota_compare_fusion.2
  14.2 0.4 convert_reduce_fusion
  14.7 0.7 add_select_fusion.1
  15.3 0.3 select_reduce_fusion.1
  15.6 0.3 fusion.2
  16.0 4.7 %gather_fusion.1 = s32[768]{0:T(1024)S(1)} fusion(s32[1,1024]{1,0:T(1,128)S(1)} %copy-done.1, s32[768]{0:T(1024)S(1)} %fusion.11), kind=kCustom, calls=%fused_computation.1 | custom fusion | bytes 12288 | tf_op jit(solution)/shard_map/gather | solution.py:64
  20.7 3.3 %gather_fusion.2 = bf16[768,512]{1,0:T(8,128)(2,1)} fusion(bf16[1024,512]{1,0:T(8,128)(2,1)S(1)} %copy-done.3, s32[1024]{0:T(1024)S(1)} %pad_clamp_fusion.1), kind=kCustom, calls=%fused_computation.2 | custom fusion | bytes 1575936 | tf_op jit(solution)/shard_map/gather | solution.py:64
  24.1 1.3 gather.23
  25.6 1.2 broadcast_select_fusion
  26.8 12.0 %all-to-all-start = ((bf16[128,6,512]{2,1,0:T(8,128)(2,1)}), bf16[128,6,512]{2,1,0:T(8,128)(2,1)}, u32[]{:S(2)}, u32[]{:S(2)}) async-start(bf16[128,6,512]{2,1,0:T(8,128)(2,1)} %broadcast_select_fusion), calls=%async_computation | async-start | bytes 2097152 | tf_op jit(solution)/shard_map/all_to_all | solution.py:66
  38.8 4.6 %select_reduce_fusion = s32[256]{0:T(256)S(1)} fusion(s32[32768]{0:T(1024)S(1)} %copy-done.2, s32[256]{0:T(256)S(1)} %iota_add_fusion), kind=kLoop, calls=%fused_computation.6 | loop fusion | flops 25165568 | bytes 133120 | tf_op jit(solution)/shard_map/reduce_sum | solution.py:76
  43.8 0.2 convert_reduce_fusion.2
  44.0 0.2 convert_reduce_fusion.1
  44.3 13.4 %all-to-all-done = bf16[128,6,512]{2,1,0:T(8,128)(2,1)} async-done(((bf16[128,6,512]{2,1,0:T(8,128)(2,1)}), bf16[128,6,512]{2,1,0:T(8,128)(2,1)}, u32[]{:S(2)}, u32[]{:S(2)}) %all-to-all-start) | async-done | bytes 786464 | tf_op jit(solution)/shard_map/all_to_all | solution.py:66
  57.7 1.4 reshape.199
  59.0 1.9 gather_fusion.3
  61.0 1.1 broadcast_in_dim.79
  62.1 30.8 %all_to_all.27 = bf16[8,256,512]{2,1,0:T(8,128)(2,1)} all-to-all(bf16[8,256,512]{2,1,0:T(8,128)(2,1)S(1)} %broadcast_in_dim.79), channel_id=1, replica_groups=mesh['row'=16,'col'=8] {'col'}, dimensions={0} | all-to-all | bytes 4194304 | tf_op jit(solution)/shard_map/all_to_all | solution.py:14
  92.9 15.8 %all-gather.3.cloned.1.call-done = bf16[4096,512]{1,0:T(8,128)(2,1)} async-done(((bf16[256,512]{1,0:T(8,128)(2,1)}), bf16[4096,512]{1,0:T(8,128)(2,1)}) %all-gather.3.cloned.1.call-update) | async-done | bytes 4194320 | tf_op jit(solution)/shard_map/all_gather | solution.py:86
  108.7 26.1 %fusion = f32[2048,512]{1,0:T(8,128)} fusion(bf16[4096,512]{1,0:T(8,128)(2,1)} %all-gather.3.cloned.1.call-done, bf16[2048,4096]{1,0:T(8,128)(2,1)} %param.8, bf16[2048,512]{1,0:T(8,128)(2,1)} %bitcast.27), kind=kOutput, calls=%fused_computation.7 | convolution fusion | flops 17213423616 | bytes 27262976 | tf_op jit(solution)/shard_map/dot_general | solution.py:35
  134.8 0.5 broadcast.260
  135.5 0.7 reduce.10
  136.2 17.2 %all_to_all.28 = s32[128,1,8]{2,1,0:T(1,128)S(1)} all-to-all(s32[128,1,8]{2,1,0:T(1,128)S(1)} %bitcast.28), channel_id=1, replica_groups=mesh['row'=16,'col'=8] {'row','col'}, dimensions={0} | all-to-all | bytes 8192 | tf_op jit(solution)/shard_map/all_to_all | solution.py:94
  153.5 16.8 %reduce-scatter.2.cloned.1.call-done = f32[256,512]{1,0:T(8,128)} async-done(((f32[2048,512]{1,0:T(8,128)}), f32[256,512]{1,0:T(8,128)}) %reduce-scatter.2.cloned.1.call-update) | async-done | bytes 524304 | tf_op jit(solution)/shard_map/reduce_scatter | solution.py:88
  170.3 1.1 convert_element_type.31
  171.4 4.0 %gather_fusion.4 = bf16[1024,512]{1,0:T(8,128)(2,1)S(1)} fusion(bf16[256,512]{1,0:T(8,128)(2,1)S(1)} %convert_element_type.31, s32[1024]{0:T(1024)S(1)} %broadcast_clamp_fusion), kind=kCustom, calls=%fused_computation.4 | custom fusion | bytes 2101248 | tf_op jit(solution)/shard_map/gather | solution.py:93
  175.4 29.2 %all_to_all.29 = bf16[128,8,512]{2,1,0:T(8,128)(2,1)S(1)} all-to-all(bf16[128,8,512]{2,1,0:T(8,128)(2,1)S(1)} %bitcast.26), channel_id=1, replica_groups=mesh['row'=16,'col'=8] {'row','col'}, dimensions={0} | all-to-all | bytes 2097152 | tf_op jit(solution)/shard_map/all_to_all | solution.py:92
  204.5 2.6 %negate_bitcast_fusion = f32[1024,512]{0,1:T(8,128)} fusion(bf16[1024,1024]{1,0:T(8,128)(2,1)S(1)} %copy-done, bf16[128,8,512]{2,1,0:T(8,128)(2,1)S(1)} %all_to_all.29), kind=kOutput, calls=%fused_computation.15 | convolution fusion | flops 1074266112 | bytes 5242880 | tf_op jit(solution)/shard_map/dot_general | solution.py:102
  207.2 2.9 %copy.17 = f32[1024,512]{1,0:T(8,128)} copy(f32[1024,512]{0,1:T(8,128)} %negate_bitcast_fusion) | data formatting | bytes 4194304 | tf_op jit(solution)/shard_map/neg | solution.py:102
  (33 shorter events, 1.1 us)
Async XLA Ops:
  6.5 198.0 %copy-start = (bf16[1024,1024]{1,0:T(8,128)(2,1)S(1)}, bf16[1024,1024]{1,0:T(8,128)(2,1)}, u32[]{:S(2)}) copy-start(bf16[1024,1024]{1,0:T(8,128)(2,1)} %param.9) | copy-start | bytes 6291460
  6.5 9.5 %copy-start.1 = (s32[1,1024]{1,0:T(1,128)S(1)}, s32[1,1024]{1,0:T(1,128)}, u32[]{:S(2)}) copy-start(s32[1,1024]{1,0:T(1,128)} %param.12) | copy-start | bytes 12292
  13.5 7.3 %copy-start.3 = (bf16[1024,512]{1,0:T(8,128)(2,1)S(1)}, bf16[1024,512]{1,0:T(8,128)(2,1)}, u32[]{:S(2)}) copy-start(bf16[1024,512]{1,0:T(8,128)(2,1)} %param.7) | copy-start | bytes 3145732
  25.4 13.4 %copy-start.2 = (s32[32768]{0:T(1024)S(1)}, s32[32768]{0:T(1024)}, u32[]{:S(2)}) copy-start(s32[32768]{0:T(1024)} %param.11) | copy-start | bytes 393220
  25.4 18.0 %copy-start.5 = (s32[128]{0:T(128)S(1)}, s32[128]{0:T(128)}, u32[]{:S(2)}) copy-start(s32[128]{0:T(128)} %param.10) | copy-start | bytes 1540
  26.8 30.9 %all-to-all-start = ((bf16[128,6,512]{2,1,0:T(8,128)(2,1)}), bf16[128,6,512]{2,1,0:T(8,128)(2,1)}, u32[]{:S(2)}, u32[]{:S(2)}) async-start(bf16[128,6,512]{2,1,0:T(8,128)(2,1)} %broadcast_select_fusion), calls=%async_computation | async-start | bytes 2097152 | tf_op jit(solution)/shard_map/all_to_all | solution.py:66
  38.7 70.0 %all-gather.3.cloned.1.call-start = ((), (), s32[]{:S(2)}) async-start(), calls=%async_computation.6 | async-start | bytes 4456448 | tf_op jit(solution)/shard_map/all_gather | solution.py:86
  60.9 109.4 %reduce-scatter.2.cloned.1.call-start = ((), (), s32[]{:S(2)}) async-start(), calls=%async_computation.5 | async-start | bytes 4718592 | tf_op jit(solution)/shard_map/reduce_scatter | solution.py:88
  134.8 0.7 copy-start.4
Sparse Core Ops, SparseCore 0:
  61.0 47.5 all-gather.2
  134.9 35.3 reduce-scatter.1
where the time goes:
time: 217 us
  blocking collectives  77.1 us (36%)
  waiting for transfers between devices  46 us (21%)
  matrix products  28.8 us (13%)
  local copies, waits for them, and re-layouts  26.3 us (12%)
  between operations  13.7 us (6%)
  other arithmetic  13 us (6%)
  starting transfers between devices  12 us (6%)
    all_to_all x1, blocking collectives, copy_for_each(): return lax.all_to_all(copies, axis, split_axis=0, concat_axis=0, tiled=True)  30.8 us
    all_to_all x1, blocking collectives, shards(): lax.all_to_all(owned_result[lax.all_to_all(wanted, ('row', 'col'), split_...  29.2 us
    dot_general x1, matrix products, add_block(): return jnp.dot(weighted, shard_rows, preferred_element_type=jnp.float32)  26.1 us
    all_to_all x1, blocking collectives, shards(): lax.all_to_all(wanted, ('row', 'col'), split_axis=0, concat_axis=0, tiled...  17.2 us
    reduce_scatter x1, waiting for transfers between devices, shards(): lax.psum_scatter(partial_sums, 'col', scatter_dimension=0, tiled=True)  16.8 us
    all_gather x1, waiting for transfers between devices, shards(): lax.all_gather(owned_rows, 'row', axis=0, tiled=True)  15.8 us
    all_to_all x1, waiting for transfers between devices, shards(): lax.all_to_all(outgoing.reshape(box_total, capacity, NORB), ('row', 'col'...  13.4 us
    all_to_all x1, starting transfers between devices, shards(): lax.all_to_all(outgoing.reshape(box_total, capacity, NORB), ('row', 'col'...  12 us
  transfers between devices with their start and end apart: 3, of which 3 were waited for; matrix products, arithmetic and copies ran while one was open for 4% of the time, Pallas kernels for 0%

commit v1 on v0

--- a/solution.py
+++ b/solution.py
@@ -7,6 +7,19 @@
 LIST = 1024
 OWN = 256
 SLOTS = 768
+
+
+def ring_gather(shard, axis, dim):
+    ways = lax.axis_size(axis)
+    up = [(d, (d + 1) % ways) for d in range(ways)]
+    down = [(d, (d - 1) % ways) for d in range(ways)]
+    earlier, later = ([shard], [shard])
+    for _ in range(ways // 2):
+        earlier.append(lax.ppermute(earlier[-1], axis, up))
+    for _ in range((ways - 1) // 2):
+        later.append(lax.ppermute(later[-1], axis, down))
+    line = jnp.concatenate([*earlier[::-1], *later[1:]], axis=dim)
+    return jnp.roll(line, (lax.axis_index(axis) - ways // 2) * shard.shape[dim], axis=dim)
 
 
 def copy_for_each(x, axis):
@@ -82,9 +95,7 @@
     source_rank = jnp.sum(earlier.astype(jnp.int32), axis=1)
     owned_rows = received[source * capacity + source_rank]
     left_rows = gather_directly(owned_rows, "col", 0)
-    partial_sums = add_block(
-        lax.all_gather(owned_rows, "row", axis=0, tiled=True), left_rows, coulomb
-    )
+    partial_sums = add_block(ring_gather(owned_rows, "row", 0), left_rows, coulomb)
     owned_result = lax.psum_scatter(partial_sums, "col", scatter_dimension=0, tiled=True).astype(
         jnp.bfloat16
     )

time: 217 us -> 287 us (1.32)
  starting transfers between devices: 12 us -> 61.5 us
  local copies, waits for them, and re-layouts: 26.3 us -> 62.7 us
  blocking collectives: 77.1 us -> 43.1 us
  waiting for transfers between devices: 46 us -> 63.1 us
    unnamed x13 -> x66, local copies, waits for them, and re-layouts: 0.69 us -> 37.1 us
    ppermute x0 -> x15, starting transfers between devices: none -> 34.7 us  [the longest x7 34.5 us: ring_gather(): later.append(lax.ppermute(later[-1], axis, down))]
    ppermute x0 -> x15, waiting for transfers between devices: none -> 32.7 us  [the longest x8 32.3 us: ring_gather(): earlier.append(lax.ppermute(earlier[-1], axis, up))]
    all_to_all x1 -> x0, blocking collectives: 30.8 us -> none  [copy_for_each(): return lax.all_to_all(copies, axis, split_axis=0, concat_axis=0, tiled=True)]
    all_gather x1 -> x0, waiting for transfers between devices: 15.8 us -> none  [shards(): lax.all_gather(owned_rows, 'row', axis=0, tiled=True)]
    all_to_all x0 -> x1, starting transfers between devices: none -> 14.8 us  [copy_for_each(): return lax.all_to_all(copies, axis, split_axis=0, concat_axis=0, tiled=True)]
    all_to_all x1, blocking collectives: 17.2 us -> 13.9 us  [shards(): lax.all_to_all(wanted, ('row', 'col'), split_axis=0, concat_axis=0, tiled...]
  transfers between devices with their start and end apart: 3 -> 18, of which waited for: 3 -> 10; matrix products, arithmetic and copies ran while one was open for 4% -> 16% of each run, Pallas kernels for 0% -> 0%
where the time goes in v1:
time: 287 us; the launch traced here: 286 us
  waiting for transfers between devices  63.1 us (22%)
  local copies, waits for them, and re-layouts  62.7 us (22%)
  starting transfers between devices  61.5 us (21%)
  blocking collectives  43.1 us (15%)
  matrix products  28.9 us (10%)
  between operations  13.7 us (5%)
  other arithmetic  12.9 us (4%)
    unnamed x66, local copies, waits for them, and re-layouts  37.1 us
    ppermute x7, starting transfers between devices, ring_gather(): later.append(lax.ppermute(later[-1], axis, down))  34.5 us
    ppermute x8, waiting for transfers between devices, ring_gather(): earlier.append(lax.ppermute(earlier[-1], axis, up))  32.3 us
    all_to_all x1, blocking collectives, shards(): lax.all_to_all(owned_result[lax.all_to_all(wanted, ('row', 'col'), split_...  29.3 us
    dot_general x1, matrix products, add_block(): return jnp.dot(weighted, shard_rows, preferred_element_type=jnp.float32)  26.2 us
    reduce_scatter x1, waiting for transfers between devices, shards(): lax.psum_scatter(partial_sums, 'col', scatter_dimension=0, tiled=True)  17 us
    all_to_all x1, starting transfers between devices, copy_for_each(): return lax.all_to_all(copies, axis, split_axis=0, concat_axis=0, tiled=True)  14.8 us
    all_to_all x1, blocking collectives, shards(): lax.all_to_all(wanted, ('row', 'col'), split_axis=0, concat_axis=0, tiled...  13.9 us
  transfers between devices with their start and end apart: 18, of which 10 were waited for; matrix products, arithmetic and copies ran while one was open for 16% of the time, Pallas kernels for 0%

profile of v1, /device:TPU:1, one launch (start us, length us, event | category | flops | bytes accessed | tf_op | source)
XLA Modules:
  0.0 285.9 jit_solution(2334102191228378859)
XLA Ops:
  8.8 4.7 %gather_fusion = s32[768]{0:T(1024)S(1)} fusion(s32[32768]{0:T(1024)} %param.11, s32[1024]{0:T(1024)S(1)} %pad_clamp_fusion.2), kind=kCustom, calls=%fused_computation | custom fusion | bytes 9216 | tf_op jit(solution)/shard_map/gather | solution.py:65
  15.9 4.2 %gather_fusion.1 = s32[768]{0:T(1024)S(1)} fusion(s32[1,1024]{1,0:T(1,128)} %param.12, s32[768]{0:T(1024)S(1)} %fusion.18), kind=kCustom, calls=%fused_computation.1 | custom fusion | bytes 12288 | tf_op jit(solution)/shard_map/gather | solution.py:77
  20.2 3.3 %gather_fusion.2 = bf16[768,512]{1,0:T(8,128)(2,1)} fusion(bf16[1024,512]{1,0:T(8,128)(2,1)S(1)} %copy-done.2, s32[1024]{0:T(1024)S(1)} %pad_clamp_fusion.1), kind=kCustom, calls=%fused_computation.2 | custom fusion | bytes 1575936 | tf_op jit(solution)/shard_map/gather | solution.py:77
  26.2 12.0 %all-to-all-start = ((bf16[128,6,512]{2,1,0:T(8,128)(2,1)}), bf16[128,6,512]{2,1,0:T(8,128)(2,1)}, u32[]{:S(2)}, u32[]{:S(2)}) async-start(bf16[128,6,512]{2,1,0:T(8,128)(2,1)} %broadcast_select_fusion), calls=%async_computation | async-start | bytes 2097152 | tf_op jit(solution)/shard_map/all_to_all | solution.py:79
  38.2 4.6 %select_reduce_fusion = s32[256]{0:T(256)S(1)} fusion(s32[32768]{0:T(1024)S(1)} %copy-done.1, s32[256]{0:T(256)S(1)} %iota_add_fusion), kind=kLoop, calls=%fused_computation.6 | loop fusion | flops 25165568 | bytes 133120 | tf_op jit(solution)/shard_map/reduce_sum | solution.py:89
  43.7 13.4 %all-to-all-done = bf16[128,6,512]{2,1,0:T(8,128)(2,1)} async-done(((bf16[128,6,512]{2,1,0:T(8,128)(2,1)}), bf16[128,6,512]{2,1,0:T(8,128)(2,1)}, u32[]{:S(2)}, u32[]{:S(2)}) %all-to-all-start) | async-done | bytes 786464 | tf_op jit(solution)/shard_map/all_to_all | solution.py:79
  59.9 9.8 %collective-permute-done = bf16[256,512]{1,0:T(8,128)(2,1)S(1)} collective-permute-done((bf16[256,512]{1,0:T(8,128)(2,1)S(1)}, bf16[256,512]{1,0:T(8,128)(2,1)S(1)}, u32[]{:S(2)}, u32[]{:S(2)}) %collective-permute-start) | collective-permute-done | bytes 262176 | tf_op jit(solution)/shard_map/ppermute | solution.py:18
  69.7 4.8 %collective-permute-start.8 = (bf16[256,512]{1,0:T(8,128)(2,1)S(1)}, bf16[256,512]{1,0:T(8,128)(2,1)S(1)}, u32[]{:S(2)}, u32[]{:S(2)}) collective-permute-start(bf16[256,512]{1,0:T(8,128)(2,1)S(1)} %gather_fusion.3), channel_id=1, source_target_pairs={{0,120},{8,0},{16,8},{24,16},{32,24},{40,32},{48,40},{56,48},{64,5... | collective-permute-start | bytes 786440 | tf_op jit(solution)/shard_map/ppermute | solution.py:20
  74.5 4.2 %collective-permute-done.1 = bf16[256,512]{1,0:T(8,128)(2,1)S(1)} collective-permute-done((bf16[256,512]{1,0:T(8,128)(2,1)S(1)}, bf16[256,512]{1,0:T(8,128)(2,1)S(1)}, u32[]{:S(2)}, u32[]{:S(2)}) %collective-permute-start.1) | collective-permute-done | bytes 262176 | tf_op jit(solution)/shard_map/ppermute | solution.py:18
  78.7 4.8 %collective-permute-start.9 = (bf16[256,512]{1,0:T(8,128)(2,1)S(1)}, bf16[256,512]{1,0:T(8,128)(2,1)S(1)}, u32[]{:S(2)}, u32[]{:S(2)}) collective-permute-start(bf16[256,512]{1,0:T(8,128)(2,1)S(1)} %collective-permute-done.8), channel_id=1, source_target_pairs={{0,120},{8,0},{16,8},{24,16},{32,24},{40,32},{48,40},{56,48},{64,5... | collective-permute-start | bytes 786440 | tf_op jit(solution)/shard_map/ppermute | solution.py:20
  83.5 3.8 %collective-permute-done.2 = bf16[256,512]{1,0:T(8,128)(2,1)S(1)} collective-permute-done((bf16[256,512]{1,0:T(8,128)(2,1)S(1)}, bf16[256,512]{1,0:T(8,128)(2,1)S(1)}, u32[]{:S(2)}, u32[]{:S(2)}) %collective-permute-start.2) | collective-permute-done | bytes 262176 | tf_op jit(solution)/shard_map/ppermute | solution.py:18
  87.3 4.8 %collective-permute-start.10 = (bf16[256,512]{1,0:T(8,128)(2,1)S(1)}, bf16[256,512]{1,0:T(8,128)(2,1)S(1)}, u32[]{:S(2)}, u32[]{:S(2)}) collective-permute-start(bf16[256,512]{1,0:T(8,128)(2,1)S(1)} %collective-permute-done.9), channel_id=1, source_target_pairs={{0,120},{8,0},{16,8},{24,16},{32,24},{40,32},{48,40},{56,48},{64,5... | collective-permute-start | bytes 786440 | tf_op jit(solution)/shard_map/ppermute | solution.py:20
  92.0 3.8 %collective-permute-done.3 = bf16[256,512]{1,0:T(8,128)(2,1)S(1)} collective-permute-done((bf16[256,512]{1,0:T(8,128)(2,1)S(1)}, bf16[256,512]{1,0:T(8,128)(2,1)S(1)}, u32[]{:S(2)}, u32[]{:S(2)}) %collective-permute-start.3) | collective-permute-done | bytes 262176 | tf_op jit(solution)/shard_map/ppermute | solution.py:18
  95.8 4.8 %collective-permute-start.11 = (bf16[256,512]{1,0:T(8,128)(2,1)S(1)}, bf16[256,512]{1,0:T(8,128)(2,1)S(1)}, u32[]{:S(2)}, u32[]{:S(2)}) collective-permute-start(bf16[256,512]{1,0:T(8,128)(2,1)S(1)} %collective-permute-done.10), channel_id=1, source_target_pairs={{0,120},{8,0},{16,8},{24,16},{32,24},{40,32},{48,40},{56,48},{64,5... | collective-permute-start | bytes 786440 | tf_op jit(solution)/shard_map/ppermute | solution.py:20
  100.6 3.7 %collective-permute-done.4 = bf16[256,512]{1,0:T(8,128)(2,1)S(1)} collective-permute-done((bf16[256,512]{1,0:T(8,128)(2,1)S(1)}, bf16[256,512]{1,0:T(8,128)(2,1)S(1)}, u32[]{:S(2)}, u32[]{:S(2)}) %collective-permute-start.4) | collective-permute-done | bytes 262176 | tf_op jit(solution)/shard_map/ppermute | solution.py:18
  105.1 4.8 %collective-permute-start.12 = (bf16[256,512]{1,0:T(8,128)(2,1)S(1)}, bf16[256,512]{1,0:T(8,128)(2,1)}, u32[]{:S(2)}, u32[]{:S(2)}) collective-permute-start(bf16[256,512]{1,0:T(8,128)(2,1)S(1)} %collective-permute-done.11), channel_id=1, source_target_pairs={{0,120},{8,0},{16,8},{24,16},{32,24},{40,32},{48,40},{56,48},{64,5... | collective-permute-start | bytes 786440 | tf_op jit(solution)/shard_map/ppermute | solution.py:20
  109.9 3.0 %collective-permute-done.5 = bf16[256,512]{1,0:T(8,128)(2,1)S(1)} collective-permute-done((bf16[256,512]{1,0:T(8,128)(2,1)S(1)}, bf16[256,512]{1,0:T(8,128)(2,1)S(1)}, u32[]{:S(2)}, u32[]{:S(2)}) %collective-permute-start.5) | collective-permute-done | bytes 262176 | tf_op jit(solution)/shard_map/ppermute | solution.py:18
  113.2 5.3 %collective-permute-start.13 = (bf16[256,512]{1,0:T(8,128)(2,1)}, bf16[256,512]{1,0:T(8,128)(2,1)}, u32[]{:S(2)}, u32[]{:S(2)}) collective-permute-start(bf16[256,512]{1,0:T(8,128)(2,1)} %collective-permute-done.12), channel_id=1, source_target_pairs={{0,120},{8,0},{16,8},{24,16},{32,24},{40,32},{48,40},{56,48},{64,5... | collective-permute-start | bytes 786440 | tf_op jit(solution)/shard_map/ppermute | solution.py:20
  118.6 4.1 %collective-permute-done.6 = bf16[256,512]{1,0:T(8,128)(2,1)} collective-permute-done((bf16[256,512]{1,0:T(8,128)(2,1)S(1)}, bf16[256,512]{1,0:T(8,128)(2,1)}, u32[]{:S(2)}, u32[]{:S(2)}) %collective-permute-start.6) | collective-permute-done | bytes 262176 | tf_op jit(solution)/shard_map/ppermute | solution.py:18
  124.2 14.8 %all-to-all-start.1 = ((bf16[8,256,512]{2,1,0:T(8,128)(2,1)}), bf16[8,256,512]{2,1,0:T(8,128)(2,1)}, u32[]{:S(2)}, u32[]{:S(2)}) async-start(bf16[8,256,512]{2,1,0:T(8,128)(2,1)} %broadcast_in_dim.79), calls=%async_computation.1 | async-start | bytes 4194304 | tf_op jit(solution)/shard_map/all_to_all | solution.py:27
  139.1 5.1 %collective-permute-start.14 = (bf16[256,512]{1,0:T(8,128)(2,1)}, bf16[256,512]{1,0:T(8,128)(2,1)S(1)}, u32[]{:S(2)}, u32[]{:S(2)}) collective-permute-start(bf16[256,512]{1,0:T(8,128)(2,1)} %collective-permute-done.13), channel_id=1, source_target_pairs={{0,120},{8,0},{16,8},{24,16},{32,24},{40,32},{48,40},{56,48},{64,5... | collective-permute-start | bytes 786440 | tf_op jit(solution)/shard_map/ppermute | solution.py:20
  150.9 1.7 constant_dynamic-update-slice_fusion.27
  152.6 1.7 constant_dynamic-update-slice_fusion.26
  157.9 1.7 constant_dynamic-update-slice_fusion.20
  159.6 1.7 constant_dynamic-update-slice_fusion.19
  180.7 26.2 %fusion = f32[2048,512]{1,0:T(8,128)} fusion(bf16[2048,4096]{1,0:T(8,128)(2,1)} %param.8, bf16[8192,512]{1,0:T(8,128)(2,1)} %constant_dynamic-update-slice_fusion, s32[]{:T(128)S(6)} %select_n.119, bf16[2048,512]{1,0:T(8,128)(2,1)} %bitcast.3), kind=kOutput, calls=%fused_computation.7 | convolution fusion | flops 17221812224 | bytes 31458304 | tf_op jit(solution)/shard_map/dot_general | solution.py:48
  208.2 13.9 %all_to_all.27 = s32[128,1,8]{2,1,0:T(1,128)S(1)} all-to-all(s32[128,1,8]{2,1,0:T(1,128)S(1)} %bitcast.17), channel_id=1, replica_groups=mesh['row'=16,'col'=8] {'row','col'}, dimensions={0} | all-to-all | bytes 8192 | tf_op jit(solution)/shard_map/all_to_all | solution.py:105
  222.2 17.0 %reduce-scatter.2.cloned.1.call-done = f32[256,512]{1,0:T(8,128)} async-done(((f32[2048,512]{1,0:T(8,128)}), f32[256,512]{1,0:T(8,128)}) %reduce-scatter.2.cloned.1.call-update) | async-done | bytes 524304 | tf_op jit(solution)/shard_map/reduce_scatter | solution.py:99
  240.3 4.0 %gather_fusion.4 = bf16[1024,512]{1,0:T(8,128)(2,1)S(1)} fusion(bf16[256,512]{1,0:T(8,128)(2,1)S(1)} %convert_element_type.31, s32[1024]{0:T(1024)S(1)} %broadcast_clamp_fusion), kind=kCustom, calls=%fused_computation.4 | custom fusion | bytes 2101248 | tf_op jit(solution)/shard_map/gather | solution.py:104
  244.2 29.3 %all_to_all.28 = bf16[128,8,512]{2,1,0:T(8,128)(2,1)S(1)} all-to-all(bf16[128,8,512]{2,1,0:T(8,128)(2,1)S(1)} %bitcast.16), channel_id=1, replica_groups=mesh['row'=16,'col'=8] {'row','col'}, dimensions={0} | all-to-all | bytes 2097152 | tf_op jit(solution)/shard_map/all_to_all | solution.py:103
  273.5 2.7 negate_bitcast_fusion
  276.2 2.9 %copy.17 = f32[1024,512]{1,0:T(8,128)} copy(f32[1024,512]{0,1:T(8,128)} %negate_bitcast_fusion) | data formatting | bytes 4194304 | tf_op jit(solution)/shard_map/neg | solution.py:113
  (115 shorter events, 45.8 us)
Async XLA Ops:
  6.5 267.0 %copy-start = (bf16[1024,1024]{1,0:T(8,128)(2,1)S(1)}, bf16[1024,1024]{1,0:T(8,128)(2,1)}, u32[]{:S(2)}) copy-start(bf16[1024,1024]{1,0:T(8,128)(2,1)} %param.9) | copy-start | bytes 6291460
  6.5 13.7 %copy-start.2 = (bf16[1024,512]{1,0:T(8,128)(2,1)S(1)}, bf16[1024,512]{1,0:T(8,128)(2,1)}, u32[]{:S(2)}) copy-start(bf16[1024,512]{1,0:T(8,128)(2,1)} %param.7) | copy-start | bytes 3145732
  15.9 22.3 %copy-start.1 = (s32[32768]{0:T(1024)S(1)}, s32[32768]{0:T(1024)}, u32[]{:S(2)}) copy-start(s32[32768]{0:T(1024)} %param.11) | copy-start | bytes 393220
  15.9 26.9 %copy-start.16 = (s32[128]{0:T(128)S(1)}, s32[128]{0:T(128)}, u32[]{:S(2)}) copy-start(s32[128]{0:T(128)} %param.10) | copy-start | bytes 1540
  26.2 30.9 %all-to-all-start = ((bf16[128,6,512]{2,1,0:T(8,128)(2,1)}), bf16[128,6,512]{2,1,0:T(8,128)(2,1)}, u32[]{:S(2)}, u32[]{:S(2)}) async-start(bf16[128,6,512]{2,1,0:T(8,128)(2,1)} %broadcast_select_fusion), calls=%async_computation | async-start | bytes 2097152 | tf_op jit(solution)/shard_map/all_to_all | solution.py:79
  59.6 10.0 %collective-permute-start = (bf16[256,512]{1,0:T(8,128)(2,1)S(1)}, bf16[256,512]{1,0:T(8,128)(2,1)S(1)}, u32[]{:S(2)}, u32[]{:S(2)}) collective-permute-start(bf16[256,512]{1,0:T(8,128)(2,1)S(1)} %gather_fusion.3), channel_id=1, source_target_pairs={{0,8},{8,16},{16,24},{24,32},{32,40},{40,48},{48,56},{56,64},{64,7... | collective-permute-start | bytes 786440 | tf_op jit(solution)/shard_map/ppermute | solution.py:18
  69.7 9.0 %collective-permute-start.1 = (bf16[256,512]{1,0:T(8,128)(2,1)S(1)}, bf16[256,512]{1,0:T(8,128)(2,1)S(1)}, u32[]{:S(2)}, u32[]{:S(2)}) collective-permute-start(bf16[256,512]{1,0:T(8,128)(2,1)S(1)} %collective-permute-done), channel_id=1, source_target_pairs={{0,8},{8,16},{16,24},{24,32},{32,40},{40,48},{48,56},{56,64},{64,7... | collective-permute-start | bytes 786440 | tf_op jit(solution)/shard_map/ppermute | solution.py:18
  69.7 9.0 %collective-permute-start.8 = (bf16[256,512]{1,0:T(8,128)(2,1)S(1)}, bf16[256,512]{1,0:T(8,128)(2,1)S(1)}, u32[]{:S(2)}, u32[]{:S(2)}) collective-permute-start(bf16[256,512]{1,0:T(8,128)(2,1)S(1)} %gather_fusion.3), channel_id=1, source_target_pairs={{0,120},{8,0},{16,8},{24,16},{32,24},{40,32},{48,40},{56,48},{64,5... | collective-permute-start | bytes 786440 | tf_op jit(solution)/shard_map/ppermute | solution.py:20
  78.7 8.5 %collective-permute-start.2 = (bf16[256,512]{1,0:T(8,128)(2,1)S(1)}, bf16[256,512]{1,0:T(8,128)(2,1)S(1)}, u32[]{:S(2)}, u32[]{:S(2)}) collective-permute-start(bf16[256,512]{1,0:T(8,128)(2,1)S(1)} %collective-permute-done.1), channel_id=1, source_target_pairs={{0,8},{8,16},{16,24},{24,32},{32,40},{40,48},{48,56},{56,64},{64,7... | collective-permute-start | bytes 786440 | tf_op jit(solution)/shard_map/ppermute | solution.py:18
  78.7 8.5 %collective-permute-start.9 = (bf16[256,512]{1,0:T(8,128)(2,1)S(1)}, bf16[256,512]{1,0:T(8,128)(2,1)S(1)}, u32[]{:S(2)}, u32[]{:S(2)}) collective-permute-start(bf16[256,512]{1,0:T(8,128)(2,1)S(1)} %collective-permute-done.8), channel_id=1, source_target_pairs={{0,120},{8,0},{16,8},{24,16},{32,24},{40,32},{48,40},{56,48},{64,5... | collective-permute-start | bytes 786440 | tf_op jit(solution)/shard_map/ppermute | solution.py:20
  87.2 8.5 %collective-permute-start.3 = (bf16[256,512]{1,0:T(8,128)(2,1)S(1)}, bf16[256,512]{1,0:T(8,128)(2,1)S(1)}, u32[]{:S(2)}, u32[]{:S(2)}) collective-permute-start(bf16[256,512]{1,0:T(8,128)(2,1)S(1)} %collective-permute-done.2), channel_id=1, source_target_pairs={{0,8},{8,16},{16,24},{24,32},{32,40},{40,48},{48,56},{56,64},{64,7... | collective-permute-start | bytes 786440 | tf_op jit(solution)/shard_map/ppermute | solution.py:18
  87.3 8.5 %collective-permute-start.10 = (bf16[256,512]{1,0:T(8,128)(2,1)S(1)}, bf16[256,512]{1,0:T(8,128)(2,1)S(1)}, u32[]{:S(2)}, u32[]{:S(2)}) collective-permute-start(bf16[256,512]{1,0:T(8,128)(2,1)S(1)} %collective-permute-done.9), channel_id=1, source_target_pairs={{0,120},{8,0},{16,8},{24,16},{32,24},{40,32},{48,40},{56,48},{64,5... | collective-permute-start | bytes 786440 | tf_op jit(solution)/shard_map/ppermute | solution.py:20
  95.8 17.4 %copy-start.9 = (bf16[256,512]{1,0:T(8,128)(2,1)}, bf16[256,512]{1,0:T(8,128)(2,1)S(1)}, u32[]{:S(2)}) copy-start(bf16[256,512]{1,0:T(8,128)(2,1)S(1)} %collective-permute-done.3) | copy-start | bytes 786436
  95.8 8.5 %collective-permute-start.4 = (bf16[256,512]{1,0:T(8,128)(2,1)S(1)}, bf16[256,512]{1,0:T(8,128)(2,1)S(1)}, u32[]{:S(2)}, u32[]{:S(2)}) collective-permute-start(bf16[256,512]{1,0:T(8,128)(2,1)S(1)} %collective-permute-done.3), channel_id=1, source_target_pairs={{0,8},{8,16},{16,24},{24,32},{32,40},{40,48},{48,56},{56,64},{64,7... | collective-permute-start | bytes 786440 | tf_op jit(solution)/shard_map/ppermute | solution.py:18
  95.8 8.5 %collective-permute-start.11 = (bf16[256,512]{1,0:T(8,128)(2,1)S(1)}, bf16[256,512]{1,0:T(8,128)(2,1)S(1)}, u32[]{:S(2)}, u32[]{:S(2)}) collective-permute-start(bf16[256,512]{1,0:T(8,128)(2,1)S(1)} %collective-permute-done.10), channel_id=1, source_target_pairs={{0,120},{8,0},{16,8},{24,16},{32,24},{40,32},{48,40},{56,48},{64,5... | collective-permute-start | bytes 786440 | tf_op jit(solution)/shard_map/ppermute | solution.py:20
  104.3 14.2 %copy-start.11 = (bf16[256,512]{1,0:T(8,128)(2,1)}, bf16[256,512]{1,0:T(8,128)(2,1)S(1)}, u32[]{:S(2)}) copy-start(bf16[256,512]{1,0:T(8,128)(2,1)S(1)} %collective-permute-done.4) | copy-start | bytes 786436
  104.3 8.6 %collective-permute-start.5 = (bf16[256,512]{1,0:T(8,128)(2,1)S(1)}, bf16[256,512]{1,0:T(8,128)(2,1)S(1)}, u32[]{:S(2)}, u32[]{:S(2)}) collective-permute-start(bf16[256,512]{1,0:T(8,128)(2,1)S(1)} %collective-permute-done.4), channel_id=1, source_target_pairs={{0,8},{8,16},{16,24},{24,32},{32,40},{40,48},{48,56},{56,64},{64,7... | collective-permute-start | bytes 786440 | tf_op jit(solution)/shard_map/ppermute | solution.py:18
  105.1 8.1 %collective-permute-start.12 = (bf16[256,512]{1,0:T(8,128)(2,1)S(1)}, bf16[256,512]{1,0:T(8,128)(2,1)}, u32[]{:S(2)}, u32[]{:S(2)}) collective-permute-start(bf16[256,512]{1,0:T(8,128)(2,1)S(1)} %collective-permute-done.11), channel_id=1, source_target_pairs={{0,120},{8,0},{16,8},{24,16},{32,24},{40,32},{48,40},{56,48},{64,5... | collective-permute-start | bytes 786440 | tf_op jit(solution)/shard_map/ppermute | solution.py:20
  112.9 9.8 %copy-start.13 = (bf16[256,512]{1,0:T(8,128)(2,1)}, bf16[256,512]{1,0:T(8,128)(2,1)S(1)}, u32[]{:S(2)}) copy-start(bf16[256,512]{1,0:T(8,128)(2,1)S(1)} %collective-permute-done.5) | copy-start | bytes 786436
  112.9 9.8 %collective-permute-start.6 = (bf16[256,512]{1,0:T(8,128)(2,1)S(1)}, bf16[256,512]{1,0:T(8,128)(2,1)}, u32[]{:S(2)}, u32[]{:S(2)}) collective-permute-start(bf16[256,512]{1,0:T(8,128)(2,1)S(1)} %collective-permute-done.5), channel_id=1, source_target_pairs={{0,8},{8,16},{16,24},{24,32},{32,40},{40,48},{48,56},{56,64},{64,7... | collective-permute-start | bytes 786440 | tf_op jit(solution)/shard_map/ppermute | solution.py:18
  113.2 25.8 %collective-permute-start.13 = (bf16[256,512]{1,0:T(8,128)(2,1)}, bf16[256,512]{1,0:T(8,128)(2,1)}, u32[]{:S(2)}, u32[]{:S(2)}) collective-permute-start(bf16[256,512]{1,0:T(8,128)(2,1)} %collective-permute-done.12), channel_id=1, source_target_pairs={{0,120},{8,0},{16,8},{24,16},{32,24},{40,32},{48,40},{56,48},{64,5... | collective-permute-start | bytes 786440 | tf_op jit(solution)/shard_map/ppermute | solution.py:20
  122.7 21.5 %collective-permute-start.7 = (bf16[256,512]{1,0:T(8,128)(2,1)}, bf16[256,512]{1,0:T(8,128)(2,1)}, u32[]{:S(2)}, u32[]{:S(2)}) collective-permute-start(bf16[256,512]{1,0:T(8,128)(2,1)} %collective-permute-done.6), channel_id=1, source_target_pairs={{0,8},{8,16},{16,24},{24,32},{32,40},{40,48},{48,56},{56,64},{64,7... | collective-permute-start | bytes 786440 | tf_op jit(solution)/shard_map/ppermute | solution.py:18
  124.2 56.5 %all-to-all-start.1 = ((bf16[8,256,512]{2,1,0:T(8,128)(2,1)}), bf16[8,256,512]{2,1,0:T(8,128)(2,1)}, u32[]{:S(2)}, u32[]{:S(2)}) async-start(bf16[8,256,512]{2,1,0:T(8,128)(2,1)} %broadcast_in_dim.79), calls=%async_computation.1 | async-start | bytes 4194304 | tf_op jit(solution)/shard_map/all_to_all | solution.py:27
  139.0 100.2 %reduce-scatter.2.cloned.1.call-start = ((), (), s32[]{:S(2)}) async-start(), calls=%async_computation.5 | async-start | bytes 4718592 | tf_op jit(solution)/shard_map/reduce_scatter | solution.py:99
  139.0 29.6 %copy-start.14 = (bf16[256,512]{1,0:T(8,128)(2,1)S(1)}, bf16[256,512]{1,0:T(8,128)(2,1)}, u32[]{:S(2)}) copy-start(bf16[256,512]{1,0:T(8,128)(2,1)} %copy-done.13) | copy-start | bytes 786436
  139.0 30.4 %copy-start.12 = (bf16[256,512]{1,0:T(8,128)(2,1)S(1)}, bf16[256,512]{1,0:T(8,128)(2,1)}, u32[]{:S(2)}) copy-start(bf16[256,512]{1,0:T(8,128)(2,1)} %copy-done.11) | copy-start | bytes 786436
  139.0 31.1 %copy-start.10 = (bf16[256,512]{1,0:T(8,128)(2,1)S(1)}, bf16[256,512]{1,0:T(8,128)(2,1)}, u32[]{:S(2)}) copy-start(bf16[256,512]{1,0:T(8,128)(2,1)} %copy-done.9) | copy-start | bytes 786436
  139.0 31.8 %copy-start.4 = (bf16[256,512]{1,0:T(8,128)(2,1)S(1)}, bf16[256,512]{1,0:T(8,128)(2,1)}, u32[]{:S(2)}) copy-start(bf16[256,512]{1,0:T(8,128)(2,1)} %copy-done.3) | copy-start | bytes 786436
  139.1 36.2 %copy-start.6 = (bf16[256,512]{1,0:T(8,128)(2,1)S(1)}, bf16[256,512]{1,0:T(8,128)(2,1)}, u32[]{:S(2)}) copy-start(bf16[256,512]{1,0:T(8,128)(2,1)} %copy-done.5) | copy-start | bytes 786436
  139.1 36.9 %copy-start.8 = (bf16[256,512]{1,0:T(8,128)(2,1)S(1)}, bf16[256,512]{1,0:T(8,128)(2,1)}, u32[]{:S(2)}) copy-start(bf16[256,512]{1,0:T(8,128)(2,1)} %copy-done.7) | copy-start | bytes 786436
  139.1 25.5 %collective-permute-start.14 = (bf16[256,512]{1,0:T(8,128)(2,1)}, bf16[256,512]{1,0:T(8,128)(2,1)S(1)}, u32[]{:S(2)}, u32[]{:S(2)}) collective-permute-start(bf16[256,512]{1,0:T(8,128)(2,1)} %collective-permute-done.13), channel_id=1, source_target_pairs={{0,120},{8,0},{16,8},{24,16},{32,24},{40,32},{48,40},{56,48},{64,5... | collective-permute-start | bytes 786440 | tf_op jit(solution)/shard_map/ppermute | solution.py:20
  180.7 26.8 %copy-start.15 = (s32[1,1024]{1,0:T(1,128)S(1)}, s32[1,1024]{1,0:T(1,128)}, u32[]{:S(2)}) copy-start(s32[1,1024]{1,0:T(1,128)} %param.13) | copy-start | bytes 12292
  (3 other events, 14.2 us)
Sparse Core Ops, SparseCore 0:
  207.1 32.0 reduce-scatter.1
